TPU v7x, 32 devices: a whole 2x2x4 slice. The times are simulated.
32 devices in a mesh: group: 2 (over x), wide: 16 (over z, y, core).
Axes of the slice: x: 2, y: 2, z: 4, core: 2. Of those that a mesh axis runs over, the one named last changes fastest.
Arguments:
- tokens: bfloat16 [192, 2688], P('group', 'wide'), parts along dimension 0, may hold values from -6 to 6
- mix_gain: bfloat16 [2688], replicated, may hold values from 0.099609375 to 1.8984375
- proj_inner: bfloat16 [2688, 2, 4096], P(None, None, 'wide'), may hold values from -0.125 to 0.125
- proj_maps: bfloat16 [2688, 2048], P(None, 'wide'), may hold values from -0.125 to 0.125
- proj_step: bfloat16 [2688, 64], P(None, 'wide'), may hold values from -0.125 to 0.125
- window_inner: bfloat16 [192, 3, 4096], P('group', None, 'wide'), parts along dimension 0, may hold values from -6 to 6
- window_maps: bfloat16 [192, 3, 2048], P('group', None, 'wide'), parts along dimension 0, may hold values from -6 to 6
- kernel_inner: bfloat16 [4, 4096], P(None, 'wide'), may hold values from -3 to 3
- kernel_maps: bfloat16 [4, 2048], P(None, 'wide'), may hold values from -3 to 3
- step_bias: float32 [64], P('wide'), may hold values from -4 to -1
- decay_log: float32 [64], P('wide'), may hold values from -1 to 2.5
- skip_gain: float32 [64], P('wide'), may hold values from 0.5 to 2
- gated_gain: bfloat16 [4096], P('wide'), may hold values from 0.099609375 to 1.8984375
- proj_out: bfloat16 [4096, 2688], P('wide'), may hold values from -0.125 to 0.125
- ssm_state: float32 [192, 64, 64, 128], P('group', 'wide'), parts along dimension 0, may hold values from -0.6 to 0.6
- moe_gain: bfloat16 [2688], replicated, may hold values from 0.099609375 to 1.8984375
- router_weight: bfloat16 [2688, 16], replicated, may hold values from -0.125 to 0.125
- expert_ids: int32 [192, 6], P('group'), parts along dimension 0, may hold values from 0 to 15, all different within a row; in each aligned block of 96 rows (0 to 95, 96 to 191, ...) at most 96 rows name the same one
- expert_up: bfloat16 [16, 2688, 928], P('wide'), may hold values from -0.125 to 0.125
- expert_down: bfloat16 [16, 928, 2688], P('wide'), may hold values from -0.1875 to 0.1875
Outputs:
- next_hidden: bfloat16 [192, 2688], P('group', 'wide'), parts along dimension 0
- new_state: float32 [192, 64, 64, 128], P('group', 'wide'), parts along dimension 0
There are 2 independent parts, one for each index of `group`. A program takes and returns all parts, laid end to end along the dimension named above; an argument that names none is the same for every part. Nothing has to cross between parts.
Inputs may be any that keep to these rules, and one draw needn't show every extreme that they name: `expert_ids`: each token names 6 different experts; no expert is named by more than 96 tokens of a part, a bound that some block reaches.
All inputs are finite; a program needn't handle non-finite values.
Results may differ from a plain program's by a relative error of at most 0.013.
Values may be sent and summed in bfloat16 or wider, within the bound.
A program may use at most 128 MiB of HBM per device.

v0:
```python
import jax
import jax.numpy as jnp
from jax import lax
from jax.sharding import PartitionSpec as P

WIDTH = 2688
HEADS = 64
HEAD_DIM = 64
STATE = 128
GROUPS = 8
TOPK = 6
INNER = 4096
epsilon = 1e-05


def rms_scale(values, axis):
    return lax.rsqrt(jnp.mean(values * values, axis=axis, keepdims=True) + epsilon)


def convolve(window, fresh, kernel):
    stacked = jnp.concatenate([window, fresh[:, None, :]], axis=1).astype(jnp.float32)
    mixed = jnp.sum(stacked * kernel.astype(jnp.float32)[None], axis=1)
    return jax.nn.silu(mixed).astype(jnp.bfloat16)


def expert_rows(rows, upward, downward):
    hidden_units = jnp.dot(rows, upward, preferred_element_type=jnp.float32)
    active = jnp.square(jnp.maximum(hidden_units, 0.0)).astype(jnp.bfloat16)
    return jnp.dot(active, downward, preferred_element_type=jnp.float32).astype(jnp.bfloat16)


def route_gates(logits, expert_ids):
    onehot = (
        expert_ids[:, :, None] == jnp.arange(logits.shape[1], dtype=jnp.int32)[None, None, :]
    ).astype(jnp.float32)
    chosen = jnp.sum(onehot * logits[:, None, :], axis=2)
    score = jax.nn.sigmoid(chosen)
    return score / jnp.sum(score, axis=1, keepdims=True)


def slot_codes(expert_ids, experts, capacity):
    flat = expert_ids.reshape(-1)
    onehot = (flat[:, None] == jnp.arange(experts, dtype=jnp.int32)[None, :]).astype(jnp.int32)
    before = jnp.cumsum(onehot, axis=0) - onehot
    slots = jnp.sum(before * onehot, axis=1)
    return (flat * capacity + slots).reshape(expert_ids.shape)


def slot_tables(codes, gates, count):
    targets = jnp.arange(count, dtype=jnp.int32)
    match = codes[None, :, :] == targets[:, None, None]
    pick = jnp.any(match, axis=2).astype(jnp.bfloat16)
    weigh = jnp.sum(jnp.where(match, gates[None], 0.0), axis=2)
    return (pick, weigh)


def local(
    tokens,
    mix_gain,
    proj_inner,
    proj_maps,
    proj_step,
    window_inner,
    window_maps,
    kernel_inner,
    kernel_maps,
    step_bias,
    decay_log,
    skip_gain,
    gated_gain,
    proj_out,
    ssm_state,
    moe_gain,
    router_weight,
    expert_ids,
    expert_up,
    expert_down,
):
    devices = lax.axis_size("wide")
    device = lax.axis_index("wide")
    seqs = tokens.shape[0]
    slice_width = tokens.shape[1]
    capacity = min(seqs, 4 * seqs * TOPK // devices)
    full_tokens = lax.all_gather(tokens, "wide", axis=1, tiled=True)
    tokens_float = full_tokens.astype(jnp.float32)
    normed = (tokens_float * rms_scale(tokens_float, 1) * mix_gain.astype(jnp.float32)).astype(
        jnp.bfloat16
    )
    local_inner = proj_inner.shape[2]
    inner = jnp.dot(
        normed, proj_inner.reshape(WIDTH, 2 * local_inner), preferred_element_type=jnp.float32
    ).astype(jnp.bfloat16)
    gate_input = inner[:, :local_inner]
    raw_inner = inner[:, local_inner:]
    maps_raw = jnp.dot(normed, proj_maps, preferred_element_type=jnp.float32).astype(jnp.bfloat16)
    step_raw = jnp.dot(normed, proj_step, preferred_element_type=jnp.float32).astype(jnp.bfloat16)
    conv_inner = convolve(window_inner, raw_inner, kernel_inner)
    conv_maps = convolve(window_maps, maps_raw, kernel_maps)
    all_maps = lax.all_gather(conv_maps, "wide", axis=1, tiled=True)
    local_heads = proj_step.shape[1]
    group = device * local_heads // (HEADS // GROUPS)
    in_maps = lax.dynamic_slice_in_dim(all_maps, group * STATE, STATE, 1).astype(jnp.float32)
    out_maps = lax.dynamic_slice_in_dim(all_maps, GROUPS * STATE + group * STATE, STATE, 1).astype(
        jnp.float32
    )
    step_size = jax.nn.softplus(step_raw.astype(jnp.float32) + step_bias)
    decay = jnp.exp(-jnp.exp(decay_log) * step_size)
    head_inputs = conv_inner.astype(jnp.float32).reshape(seqs, local_heads, HEAD_DIM)
    driven = (step_size[:, :, None] * head_inputs)[..., None] * in_maps[:, None, None, :]
    new_state = decay[:, :, None, None] * ssm_state + driven
    readout = (
        jnp.einsum("shpn,sn->shp", new_state, out_maps, precision=lax.Precision.HIGHEST)
        + skip_gain[None, :, None] * head_inputs
    )
    gated = readout.reshape(seqs, local_inner) * jax.nn.silu(gate_input.astype(jnp.float32))
    group_mask = (jnp.arange(GROUPS, dtype=jnp.int32) == group).astype(jnp.float32)
    partial_squares = jnp.sum(gated * gated, axis=1)[:, None] * group_mask[None, :]
    group_squares = lax.psum(partial_squares, "wide")
    own_squares = jnp.sum(group_squares * group_mask[None, :], axis=1, keepdims=True)
    norm_scale = lax.rsqrt(own_squares / (INNER // GROUPS) + epsilon)
    gated_out = (gated * norm_scale * gated_gain.astype(jnp.float32)).astype(jnp.bfloat16)
    mixer_terms = jnp.dot(gated_out, proj_out, preferred_element_type=jnp.float32)
    codes = slot_codes(expert_ids, devices, capacity)
    mixer_slice = lax.psum_scatter(mixer_terms, "wide", scatter_dimension=1, tiled=True)
    hidden_round = (tokens.astype(jnp.float32) + mixer_slice).astype(jnp.bfloat16)
    hidden_slice = lax.optimization_barrier(hidden_round).astype(jnp.float32)
    gain_slice = lax.dynamic_slice_in_dim(moe_gain, device * slice_width, slice_width, 0).astype(
        jnp.float32
    )
    router_slice = lax.dynamic_slice_in_dim(
        router_weight, device * slice_width, slice_width, 0
    ).astype(jnp.float32)
    weighted = hidden_slice * gain_slice
    squares, part_logits = lax.psum(
        (
            jnp.sum(hidden_slice * hidden_slice, axis=1),
            jnp.dot(weighted, router_slice, precision=lax.Precision.HIGHEST),
        ),
        "wide",
    )
    moe_scale = lax.rsqrt(squares[:, None] / WIDTH + epsilon)
    gates = route_gates(part_logits * moe_scale, expert_ids)
    moe_input = (hidden_slice * moe_scale * gain_slice).astype(jnp.bfloat16)
    pick, weigh = slot_tables(codes, gates, devices * capacity)
    sent = (
        jnp.dot(pick, moe_input, preferred_element_type=jnp.float32)
        .astype(jnp.bfloat16)
        .reshape(devices, capacity, slice_width)
    )
    served = expert_rows(
        lax.all_to_all(sent, "wide", split_axis=0, concat_axis=2, tiled=True)[0],
        expert_up[0],
        expert_down[0],
    )
    returned = lax.all_to_all(served[None], "wide", split_axis=2, concat_axis=0, tiled=True)
    moe_slice = jnp.dot(
        weigh.T,
        returned.reshape(devices * capacity, slice_width).astype(jnp.float32),
        precision=lax.Precision.HIGHEST,
    )
    next_hidden = (hidden_slice + moe_slice).astype(jnp.bfloat16)
    return (next_hidden, new_state)


def solution(mesh):
    in_specs = (
        P("group", "wide"),
        P(),
        P(None, None, "wide"),
        P(None, "wide"),
        P(None, "wide"),
        P("group", None, "wide"),
        P("group", None, "wide"),
        P(None, "wide"),
        P(None, "wide"),
        P("wide"),
        P("wide"),
        P("wide"),
        P("wide"),
        P("wide", None),
        P("group", "wide", None, None),
        P(),
        P(),
        P("group", None),
        P("wide", None, None),
        P("wide", None, None),
    )
    out_specs = (P("group", "wide"), P("group", "wide", None, None))
    return jax.shard_map(local, mesh=mesh, in_specs=in_specs, out_specs=out_specs, check_vma=False)
```

profile of v0, /device:TPU:0, one launch (start us, length us, event | category | flops | bytes accessed | tf_op | source)
XLA Modules:
  0.0 292.7 jit_solution(6536486973410003831)
XLA Ops:
  7.3 25.6 %all_gather.6 = bf16[96,2688]{0,1:T(8,128)(2,1)S(1)} all-gather(bf16[96,168]{0,1:T(8,128)(2,1)} %param.20), channel_id=1, replica_groups=mesh['group'=2,'wide'=16] {'wide'}, dimensions={1}, use_global_device_ids=true | all-gather | bytes 548352 | tf_op jit(solution)/shard_map/all_gather | solution.py:84
  33.3 0.7 convert_element_type.109
  34.0 0.7 convert_element_type.120
  34.6 1.8 fusion.24
  36.6 18.5 %all_gather.7 = bf16[96,2048]{1,0:T(8,128)(2,1)S(1)} all-gather(bf16[96,128]{1,0:T(8,128)(2,1)S(1)} %multiply_convert_fusion.3), channel_id=1, replica_groups=mesh['group'=2,'wide'=16] {'wide'}, dimensions={1}, use_global_device_ids=true | all-gather | bytes 417792 | tf_op jit(solution)/shard_map/all_gather | solution.py:99
  55.6 1.2 convolution_convert_fusion.1
  57.9 7.0 %multiply_add_fusion = f32[96,4,64,128]{3,2,1,0:T(8,128)S(1)} fusion(f32[96,4,64,128]{3,2,1,0:T(8,128)} %param.34, f32[96,128]{1,0:T(8,128)S(1)} %get-tuple-element.5, f32[96,4,64]{2,1,0:T(4,128)S(1)} %copy.72, f32[96,4]{1,0:T(8,128)S(1)} %copy.70), kind=kLoop, calls=%fused_computation | loop fusion | flops 9437184 | bytes 25314816 | tf_op jit(solution)/shard_map/add | solution.py:110
  64.9 4.8 %copy-done.1 = f32[96,4,64,128]{3,2,1,0:T(8,128)} copy-done((f32[96,4,64,128]{3,2,1,0:T(8,128)}, f32[96,4,64,128]{3,2,1,0:T(8,128)S(1)}, u32[]{:S(2)}) %copy-start.1) | copy-done | bytes 12582936
  69.7 14.7 %fusion.40 = f32[96,1,4,64]{3,1,2,0:T(1,128)S(1)} fusion(f32[96,4,64,128]{3,2,1,0:T(8,128)S(1)} %multiply_add_fusion, bf16[96,128,1,1]{1,0,2,3:T(8,128)(2,1)S(1)} %get-tuple-element.4), kind=kOutput, calls=%fused_computation.52 | convolution fusion | flops 37748736 | bytes 12705792 | tf_op jit(solution)/shard_map/shpn,sn->shp/dot_general | solution.py:112
  84.9 31.1 %psum.21 = f32[96,8]{0,1:T(8,128)S(1)} all-reduce(f32[96,8]{0,1:T(8,128)S(1)} %broadcast_multiply_fusion.1), channel_id=1, replica_groups=mesh['group'=2,'wide'=16] {'wide'}, use_global_device_ids=true, to_apply=%region_4.5 | all-reduce | flops 768 | bytes 6144 | tf_op jit(solution)/shard_map/psum | solution.py:118
  116.1 1.8 fusion.39
  118.2 1.7 reduce-window.6
  120.4 0.8 dynamic-slice_convert_fusion.1
  121.2 0.6 fusion.4
  121.9 50.8 %reduce-scatter.4.cloned.1.call-done = f32[96,168]{0,1:T(8,128)} async-done(((f32[96,2688]{0,1:T(8,128)}), f32[96,168]{0,1:T(8,128)}) %reduce-scatter.4.cloned.1.call-update) | async-done | bytes 64528
  172.7 0.9 add_convert_fusion
  173.6 0.9 fusion.35
  174.5 30.5 %all-reduce.2 = (f32[96,16]{0,1:T(8,128)S(1)}, f32[96]{0:T(128)S(1)}) all-reduce(f32[96,16]{0,1:T(8,128)S(1)} %fusion.35, f32[96]{0:T(128)S(1)} %fusion.36), channel_id=1, replica_groups=mesh['group'=2,'wide'=16] {'wide'}, use_global_device_ids=true, to_apply=%region_10.11 | all-reduce | flops 1632 | bytes 13056 | tf_op jit(solution)/shard_map/psum | solution.py:134
  205.4 0.6 reshape.115
  206.1 21.2 %all_to_all.30 = bf16[16,96,168]{1,2,0:T(8,128)(2,1)S(1)} all-to-all(bf16[16,96,168]{1,2,0:T(8,128)(2,1)S(1)} %copy.78), channel_id=1, replica_groups=mesh['group'=2,'wide'=16] {'wide'}, dimensions={0} | all-to-all | bytes 1032192 | tf_op jit(solution)/shard_map/all_to_all | solution.py:151
  227.4 6.5 %fusion.8 = bf16[1,96,2688]{2,1,0:T(8,128)(2,1)S(1)} fusion(bf16[1,928,2688]{2,1,0:T(8,128)(2,1)} %param.39, bf16[96,2688]{0,1:T(8,128)(2,1)S(1)} %bitcast.74, bf16[1,2688,928]{1,2,0:T(8,128)(2,1)} %param.38), kind=kOutput, calls=%fused_computation.9 | convolution fusion | flops 958399488 | bytes 11010048 | tf_op jit(solution)/shard_map/dot_general | solution.py:29
  233.9 1.9 copy.80
  236.3 14.9 %reduce.2 = bf16[2688,96]{1,0:T(8,128)(2,1)S(1)} reduce(bf16[2688,1,96]{2,1,0:T(2,128)(2,1)S(1)} %bitcast.70, bf16[]{:T(256)} %broadcast.123), dimensions={1}, to_apply=%bitcast.55.reduce_sub_computation | reduce | bytes 1032194
  251.3 1.9 reshape.122
  253.2 4.5 %all-to-all-start.1 = ((bf16[16,2,8064]{2,1,0:T(2,128)(2,1)}), bf16[16,2,8064]{2,1,0:T(2,128)(2,1)}, u32[]{:S(2)}, u32[]{:S(2)}) async-start(bf16[16,2,8064]{2,1,0:T(2,128)(2,1)} %reshape.122), calls=%async_computation.1 | async-start | bytes 1032192 | tf_op jit(solution)/shard_map/all_to_all | solution.py:155
  258.3 13.3 %all-to-all-done.1 = bf16[16,2,8064]{2,1,0:T(2,128)(2,1)} async-done(((bf16[16,2,8064]{2,1,0:T(2,128)(2,1)}), bf16[16,2,8064]{2,1,0:T(2,128)(2,1)}, u32[]{:S(2)}, u32[]{:S(2)}) %all-to-all-start.1) | async-done | bytes 516128 | tf_op jit(solution)/shard_map/all_to_all | solution.py:155
  271.6 5.0 %reshape.123 = bf16[2688,1,96]{2,1,0:T(2,128)(2,1)S(1)} reshape(bf16[16,2,8064]{2,1,0:T(2,128)(2,1)} %all-to-all-done.1) | data formatting | bytes 1032192
  276.6 2.8 copy.81
  279.4 3.3 %all_to_all.26 = bf16[1,96,16,168]{3,2,1,0:T(8,128)(2,1)S(1)} reshape(bf16[1,96,2688]{2,1,0:T(8,128)(2,1)} %copy.81) | data formatting | bytes 1032192 | tf_op jit(solution)/shard_map/all_to_all | solution.py:155
  282.7 1.2 copy.82
  283.9 0.7 reshape.116
  284.6 1.2 fusion.23
  (72 shorter events, 5.1 us)
Async XLA Ops:
  7.2 108.9 %copy-start = (bf16[256,2688]{1,0:T(8,128)(2,1)S(1)}, bf16[256,2688]{1,0:T(8,128)(2,1)}, u32[]{:S(2)}) copy-start(bf16[256,2688]{1,0:T(8,128)(2,1)} %param.33) | copy-start | bytes 4128772
  7.2 29.3 %copy-start.5 = (bf16[96,3,128]{2,0,1:T(8,128)(2,1)S(1)}, bf16[96,3,128]{2,0,1:T(8,128)(2,1)}, u32[]{:S(2)}) copy-start(bf16[96,3,128]{2,0,1:T(8,128)(2,1)} %param.26) | copy-start | bytes 221188
  7.2 165.5 %reduce-scatter.4.cloned.1.call-start = ((), (), s32[]{:S(2)}) async-start(), calls=%async_computation.3 | async-start | bytes 1462272
  7.3 47.8 %copy-start.2 = (bf16[2688,2,256]{2,1,0:T(2,128)(2,1)S(1)}, bf16[2688,2,256]{2,1,0:T(2,128)(2,1)}, u32[]{:S(2)}) copy-start(bf16[2688,2,256]{2,1,0:T(2,128)(2,1)} %param.22) | copy-start | bytes 8257540
  55.5 1.3 copy-start.7
  55.6 1.3 copy-start.4
  55.6 1.4 copy-start.10
  55.6 1.4 copy-start.9
  55.6 1.4 copy-start.11
  64.9 4.8 %copy-start.1 = (f32[96,4,64,128]{3,2,1,0:T(8,128)}, f32[96,4,64,128]{3,2,1,0:T(8,128)S(1)}, u32[]{:S(2)}) copy-start(f32[96,4,64,128]{3,2,1,0:T(8,128)S(1)} %multiply_add_fusion) | copy-start | bytes 37748740
  69.7 14.8 %copy-start.8 = (f32[4]{0:T(128)S(1)}, f32[4]{0:T(128)}, u32[]{:S(2)}) copy-start(f32[4]{0:T(128)} %param.31) | copy-start | bytes 52
  69.7 46.4 %copy-start.12 = (bf16[256]{0:T(256)(128)(2,1)S(1)}, bf16[256]{0:T(256)(128)(2,1)}, u32[]{:S(2)}) copy-start(bf16[256]{0:T(256)(128)(2,1)} %param.32) | copy-start | bytes 1540
  84.4 33.6 %copy-start.6 = (s32[96,6]{0,1:T(8,128)S(1)}, s32[96,6]{0,1:T(8,128)}, u32[]{:S(2)}) copy-start(s32[96,6]{0,1:T(8,128)} %param.37) | copy-start | bytes 6916
  84.6 88.1 %copy-start.3 = (bf16[96,168]{0,1:T(8,128)(2,1)S(1)}, bf16[96,168]{0,1:T(8,128)(2,1)}, u32[]{:S(2)}) copy-start(bf16[96,168]{0,1:T(8,128)(2,1)} %param.20) | copy-start | bytes 96772
  253.2 18.4 %all-to-all-start.1 = ((bf16[16,2,8064]{2,1,0:T(2,128)(2,1)}), bf16[16,2,8064]{2,1,0:T(2,128)(2,1)}, u32[]{:S(2)}, u32[]{:S(2)}) async-start(bf16[16,2,8064]{2,1,0:T(2,128)(2,1)} %reshape.122), calls=%async_computation.1 | async-start | bytes 1032192 | tf_op jit(solution)/shard_map/all_to_all | solution.py:155
Sparse Core Ops, SparseCore 0:
  118.0 54.5 reduce-scatter.3
where the time goes:
time: 293 us
  blocking collectives  127 us (43%)
  waiting for transfers between devices  64.1 us (22%)
  other arithmetic  29 us (10%)
  matrix products  29 us (10%)
  local copies, waits for them, and re-layouts  24.6 us (8%)
  between operations  14.5 us (5%)
  starting transfers between devices  4.53 us (2%)
    unnamed x2, waiting for transfers between devices  50.8 us
    psum x1, blocking collectives, local(): group_squares = lax.psum(partial_squares, 'wide')  31.1 us
    psum x1, blocking collectives, local(): lax.psum((jnp.sum(hidden_slice * hidden_slice, axis=1), jnp.dot(weighted,...  30.5 us
    all_gather x1, blocking collectives, local(): full_tokens = lax.all_gather(tokens, 'wide', axis=1, tiled=True)  25.6 us
    all_to_all x1, blocking collectives, local(): lax.all_to_all(sent, 'wide', split_axis=0, concat_axis=2, tiled=True)[0]  21.2 us
    all_gather x1, blocking collectives, local(): all_maps = lax.all_gather(conv_maps, 'wide', axis=1, tiled=True)  18.5 us
    unnamed x1, other arithmetic  14.9 us
    dot_general x1, matrix products, local(): jnp.einsum('shpn,sn->shp', new_state, out_maps, precision=lax.Precision.H...  14.7 us
  transfers between devices with their start and end apart: 2, of which 2 were waited for; matrix products, arithmetic and copies ran while one was open for 2% of the time, Pallas kernels for 0%

commit v1 on v0

--- a/solution.py
+++ b/solution.py
@@ -115,7 +115,11 @@
     gated = readout.reshape(seqs, local_inner) * jax.nn.silu(gate_input.astype(jnp.float32))
     group_mask = (jnp.arange(GROUPS, dtype=jnp.int32) == group).astype(jnp.float32)
     partial_squares = jnp.sum(gated * gated, axis=1)[:, None] * group_mask[None, :]
-    group_squares = lax.psum(partial_squares, "wide")
+    group_squares = partial_squares
+    for hop in (1, 2, 4, 8):
+        group_squares = group_squares + lax.ppermute(
+            group_squares, "wide", [(dev, dev ^ hop) for dev in range(16)]
+        )
     own_squares = jnp.sum(group_squares * group_mask[None, :], axis=1, keepdims=True)
     norm_scale = lax.rsqrt(own_squares / (INNER // GROUPS) + epsilon)
     gated_out = (gated * norm_scale * gated_gain.astype(jnp.float32)).astype(jnp.bfloat16)

time: 293 us -> 276 us (0.942)
  blocking collectives: 127 us -> 95.8 us
  waiting for transfers between devices: 64.1 us -> 76.1 us
    psum x1 -> x0, blocking collectives: 31.1 us -> none  [local(): group_squares = lax.psum(partial_squares, 'wide')]
    ppermute x0 -> x4, waiting for transfers between devices: none -> 10.8 us  [local(): lax.ppermute(group_squares, 'wide', [(dev, dev ^ hop) for dev in range(16)])]
  transfers between devices with their start and end apart: 2 -> 6, of which waited for: 2 -> 6; matrix products, arithmetic and copies ran while one was open for 2% -> 2% of each run, Pallas kernels for 0% -> 0%
where the time goes in v1:
time: 276 us
  blocking collectives  95.8 us (35%)
  waiting for transfers between devices  76.1 us (28%)
  other arithmetic  29.1 us (11%)
  matrix products  29 us (11%)
  local copies, waits for them, and re-layouts  24.6 us (9%)
  between operations  14.5 us (5%)
  starting transfers between devices  6.55 us (2%)
    unnamed x2, waiting for transfers between devices  51.9 us
    psum x1, blocking collectives, local(): lax.psum((jnp.sum(hidden_slice * hidden_slice, axis=1), jnp.dot(weighted,...  30.5 us
    all_gather x1, blocking collectives, local(): full_tokens = lax.all_gather(tokens, 'wide', axis=1, tiled=True)  25.6 us
    all_to_all x1, blocking collectives, local(): lax.all_to_all(sent, 'wide', split_axis=0, concat_axis=2, tiled=True)[0]  21.2 us
    all_gather x1, blocking collectives, local(): all_maps = lax.all_gather(conv_maps, 'wide', axis=1, tiled=True)  18.5 us
    unnamed x1, other arithmetic  14.9 us
    dot_general x1, matrix products, local(): jnp.einsum('shpn,sn->shp', new_state, out_maps, precision=lax.Precision.H...  14.7 us
    all_to_all x1, waiting for transfers between devices, local(): lax.all_to_all(served[None], 'wide', split_axis=2, concat_axis=0, tiled=T...  13.3 us
  transfers between devices with their start and end apart: 6, of which 6 were waited for; matrix products, arithmetic and copies ran while one was open for 2% of the time, Pallas kernels for 0%

profile of v1, /device:TPU:0, one launch (start us, length us, event | category | flops | bytes accessed | tf_op | source)
XLA Modules:
  0.0 275.8 jit_solution(3391873556471802510)
XLA Ops:
  7.3 25.6 %all_gather.6 = bf16[96,2688]{0,1:T(8,128)(2,1)S(1)} all-gather(bf16[96,168]{0,1:T(8,128)(2,1)} %param.20), channel_id=1, replica_groups=mesh['group'=2,'wide'=16] {'wide'}, dimensions={1}, use_global_device_ids=true | all-gather | bytes 548352 | tf_op jit(solution)/shard_map/all_gather | solution.py:84
  34.6 1.8 fusion.24
  36.6 18.5 %all_gather.7 = bf16[96,2048]{1,0:T(8,128)(2,1)S(1)} all-gather(bf16[96,128]{1,0:T(8,128)(2,1)S(1)} %multiply_convert_fusion.3), channel_id=1, replica_groups=mesh['group'=2,'wide'=16] {'wide'}, dimensions={1}, use_global_device_ids=true | all-gather | bytes 417792 | tf_op jit(solution)/shard_map/all_gather | solution.py:99
  55.6 1.2 convolution_convert_fusion.1
  57.9 7.0 %multiply_add_fusion = f32[96,4,64,128]{3,2,1,0:T(8,128)S(1)} fusion(f32[96,4,64,128]{3,2,1,0:T(8,128)} %param.34, f32[96,128]{1,0:T(8,128)S(1)} %get-tuple-element.5, f32[96,4,64]{2,1,0:T(4,128)S(1)} %copy.72, f32[96,4]{1,0:T(8,128)S(1)} %copy.70), kind=kLoop, calls=%fused_computation | loop fusion | flops 9437184 | bytes 25314816 | tf_op jit(solution)/shard_map/add | solution.py:110
  64.9 4.8 %copy-done.1 = f32[96,4,64,128]{3,2,1,0:T(8,128)} copy-done((f32[96,4,64,128]{3,2,1,0:T(8,128)}, f32[96,4,64,128]{3,2,1,0:T(8,128)S(1)}, u32[]{:S(2)}) %copy-start.1) | copy-done | bytes 12582936
  69.7 14.7 %fusion.40 = f32[96,1,4,64]{3,1,2,0:T(1,128)S(1)} fusion(f32[96,4,64,128]{3,2,1,0:T(8,128)S(1)} %multiply_add_fusion, bf16[96,128,1,1]{1,0,2,3:T(8,128)(2,1)S(1)} %get-tuple-element.4), kind=kOutput, calls=%fused_computation.52 | convolution fusion | flops 37748736 | bytes 12705792 | tf_op jit(solution)/shard_map/shpn,sn->shp/dot_general | solution.py:112
  85.3 0.8 collective-permute-done
  86.2 1.7 collective-permute-start.1
  87.8 1.9 collective-permute-done.1
  89.8 3.6 %collective-permute-done.2 = f32[96,8]{0,1:T(8,128)S(1)} collective-permute-done((f32[96,8]{0,1:T(8,128)S(1)}, f32[96,8]{0,1:T(8,128)S(1)}, u32[]{:S(2)}, u32[]{:S(2)}) %collective-permute-start.2) | collective-permute-done | bytes 3104 | tf_op jit(solution)/shard_map/ppermute | solution.py:120
  93.5 4.5 %collective-permute-done.3 = f32[96,8]{0,1:T(8,128)S(1)} collective-permute-done((f32[96,8]{0,1:T(8,128)S(1)}, f32[96,8]{0,1:T(8,128)S(1)}, u32[]{:S(2)}, u32[]{:S(2)}) %collective-permute-start.3) | collective-permute-done | bytes 3104 | tf_op jit(solution)/shard_map/ppermute | solution.py:120
  98.1 1.8 fusion.39
  100.1 1.7 reduce-window.6
  102.4 0.8 dynamic-slice_convert_fusion.1
  103.8 51.9 %reduce-scatter.4.cloned.1.call-done = f32[96,168]{0,1:T(8,128)} async-done(((f32[96,2688]{0,1:T(8,128)}), f32[96,168]{0,1:T(8,128)}) %reduce-scatter.4.cloned.1.call-update) | async-done | bytes 64528
  155.7 0.9 add_convert_fusion
  156.7 0.9 fusion.35
  157.6 30.5 %all-reduce.2 = (f32[96,16]{0,1:T(8,128)S(1)}, f32[96]{0:T(128)S(1)}) all-reduce(f32[96,16]{0,1:T(8,128)S(1)} %fusion.35, f32[96]{0:T(128)S(1)} %fusion.36), channel_id=1, replica_groups=mesh['group'=2,'wide'=16] {'wide'}, use_global_device_ids=true, to_apply=%region_9.10 | all-reduce | flops 1632 | bytes 13056 | tf_op jit(solution)/shard_map/psum | solution.py:138
  189.2 21.2 %all_to_all.30 = bf16[16,96,168]{1,2,0:T(8,128)(2,1)S(1)} all-to-all(bf16[16,96,168]{1,2,0:T(8,128)(2,1)S(1)} %copy.78), channel_id=1, replica_groups=mesh['group'=2,'wide'=16] {'wide'}, dimensions={0} | all-to-all | bytes 1032192 | tf_op jit(solution)/shard_map/all_to_all | solution.py:155
  210.4 6.5 %fusion.8 = bf16[1,96,2688]{2,1,0:T(8,128)(2,1)S(1)} fusion(bf16[1,928,2688]{2,1,0:T(8,128)(2,1)} %param.39, bf16[96,2688]{0,1:T(8,128)(2,1)S(1)} %bitcast.74, bf16[1,2688,928]{1,2,0:T(8,128)(2,1)} %param.38), kind=kOutput, calls=%fused_computation.9 | convolution fusion | flops 958399488 | bytes 11010048 | tf_op jit(solution)/shard_map/dot_general | solution.py:29
  217.0 1.9 copy.80
  219.4 14.9 %reduce.2 = bf16[2688,96]{1,0:T(8,128)(2,1)S(1)} reduce(bf16[2688,1,96]{2,1,0:T(2,128)(2,1)S(1)} %bitcast.70, bf16[]{:T(256)} %broadcast.123), dimensions={1}, to_apply=%bitcast.55.reduce_sub_computation | reduce | bytes 1032194
  234.3 1.9 reshape.122
  236.3 4.5 %all-to-all-start.1 = ((bf16[16,2,8064]{2,1,0:T(2,128)(2,1)}), bf16[16,2,8064]{2,1,0:T(2,128)(2,1)}, u32[]{:S(2)}, u32[]{:S(2)}) async-start(bf16[16,2,8064]{2,1,0:T(2,128)(2,1)} %reshape.122), calls=%async_computation.1 | async-start | bytes 1032192 | tf_op jit(solution)/shard_map/all_to_all | solution.py:159
  241.4 13.3 %all-to-all-done.1 = bf16[16,2,8064]{2,1,0:T(2,128)(2,1)} async-done(((bf16[16,2,8064]{2,1,0:T(2,128)(2,1)}), bf16[16,2,8064]{2,1,0:T(2,128)(2,1)}, u32[]{:S(2)}, u32[]{:S(2)}) %all-to-all-start.1) | async-done | bytes 516128 | tf_op jit(solution)/shard_map/all_to_all | solution.py:159
  254.7 5.0 %reshape.123 = bf16[2688,1,96]{2,1,0:T(2,128)(2,1)S(1)} reshape(bf16[16,2,8064]{2,1,0:T(2,128)(2,1)} %all-to-all-done.1) | data formatting | bytes 1032192
  259.7 2.8 %copy.81 = bf16[1,96,2688]{2,1,0:T(8,128)(2,1)} copy(bf16[1,96,2688]{1,0,2:T(2,128)(2,1)S(1)} %bitcast.71) | data formatting | bytes 1032192 | tf_op jit(solution)/shard_map/all_to_all | solution.py:159
  262.4 3.3 %all_to_all.26 = bf16[1,96,16,168]{3,2,1,0:T(8,128)(2,1)S(1)} reshape(bf16[1,96,2688]{2,1,0:T(8,128)(2,1)} %copy.81) | data formatting | bytes 1032192 | tf_op jit(solution)/shard_map/all_to_all | solution.py:159
  265.8 1.2 copy.82
  266.9 0.7 reshape.116
  267.7 1.2 fusion.23
  (82 shorter events, 8.2 us)
Async XLA Ops:
  7.2 90.9 %copy-start = (bf16[256,2688]{1,0:T(8,128)(2,1)S(1)}, bf16[256,2688]{1,0:T(8,128)(2,1)}, u32[]{:S(2)}) copy-start(bf16[256,2688]{1,0:T(8,128)(2,1)} %param.33) | copy-start | bytes 4128772
  7.2 29.3 %copy-start.5 = (bf16[96,3,128]{2,0,1:T(8,128)(2,1)S(1)}, bf16[96,3,128]{2,0,1:T(8,128)(2,1)}, u32[]{:S(2)}) copy-start(bf16[96,3,128]{2,0,1:T(8,128)(2,1)} %param.26) | copy-start | bytes 221188
  7.2 148.5 %reduce-scatter.4.cloned.1.call-start = ((), (), s32[]{:S(2)}) async-start(), calls=%async_computation.3 | async-start | bytes 1462272
  7.3 47.8 %copy-start.2 = (bf16[2688,2,256]{2,1,0:T(2,128)(2,1)S(1)}, bf16[2688,2,256]{2,1,0:T(2,128)(2,1)}, u32[]{:S(2)}) copy-start(bf16[2688,2,256]{2,1,0:T(2,128)(2,1)} %param.22) | copy-start | bytes 8257540
  55.5 1.3 copy-start.7
  55.6 1.3 copy-start.4
  55.6 1.4 copy-start.10
  55.6 1.4 copy-start.9
  55.6 1.4 copy-start.11
  64.9 4.8 %copy-start.1 = (f32[96,4,64,128]{3,2,1,0:T(8,128)}, f32[96,4,64,128]{3,2,1,0:T(8,128)S(1)}, u32[]{:S(2)}) copy-start(f32[96,4,64,128]{3,2,1,0:T(8,128)S(1)} %multiply_add_fusion) | copy-start | bytes 37748740
  69.7 14.8 %copy-start.8 = (f32[4]{0:T(128)S(1)}, f32[4]{0:T(128)}, u32[]{:S(2)}) copy-start(f32[4]{0:T(128)} %param.31) | copy-start | bytes 52
  69.7 23.8 %copy-start.12 = (bf16[256]{0:T(256)(128)(2,1)S(1)}, bf16[256]{0:T(256)(128)(2,1)}, u32[]{:S(2)}) copy-start(bf16[256]{0:T(256)(128)(2,1)} %param.32) | copy-start | bytes 1540
  84.4 15.5 %copy-start.6 = (s32[96,6]{0,1:T(8,128)S(1)}, s32[96,6]{0,1:T(8,128)}, u32[]{:S(2)}) copy-start(s32[96,6]{0,1:T(8,128)} %param.37) | copy-start | bytes 6916
  84.6 71.1 %copy-start.3 = (bf16[96,168]{0,1:T(8,128)(2,1)S(1)}, bf16[96,168]{0,1:T(8,128)(2,1)}, u32[]{:S(2)}) copy-start(bf16[96,168]{0,1:T(8,128)(2,1)} %param.20) | copy-start | bytes 96772
  84.9 1.2 collective-permute-start
  86.2 3.6 %collective-permute-start.1 = (f32[96,8]{0,1:T(8,128)S(1)}, f32[96,8]{0,1:T(8,128)S(1)}, u32[]{:S(2)}, u32[]{:S(2)}) collective-permute-start(f32[96,8]{0,1:T(8,128)S(1)} %fusion.51), channel_id=1, source_target_pairs={{0,2},{1,3},{2,0},{3,1},{4,6},{5,7},{6,4},{7,5},{8,10},{9,11},{10,... | collective-permute-start | bytes 9224 | tf_op jit(solution)/shard_map/ppermute | solution.py:120
  89.8 3.6 %collective-permute-start.2 = (f32[96,8]{0,1:T(8,128)S(1)}, f32[96,8]{0,1:T(8,128)S(1)}, u32[]{:S(2)}, u32[]{:S(2)}) collective-permute-start(f32[96,8]{0,1:T(8,128)S(1)} %fusion.67), channel_id=1, source_target_pairs={{0,4},{1,5},{2,6},{3,7},{4,0},{5,1},{6,2},{7,3},{8,12},{9,13},{10,... | collective-permute-start | bytes 9224 | tf_op jit(solution)/shard_map/ppermute | solution.py:120
  93.4 4.5 %collective-permute-start.3 = (f32[96,8]{0,1:T(8,128)S(1)}, f32[96,8]{0,1:T(8,128)S(1)}, u32[]{:S(2)}, u32[]{:S(2)}) collective-permute-start(f32[96,8]{0,1:T(8,128)S(1)} %add.116), channel_id=1, source_target_pairs={{0,8},{1,9},{2,10},{3,11},{4,12},{5,13},{6,14},{7,15},{8,0},{9,1},... | collective-permute-start | bytes 9224 | tf_op jit(solution)/shard_map/ppermute | solution.py:120
  236.3 18.4 %all-to-all-start.1 = ((bf16[16,2,8064]{2,1,0:T(2,128)(2,1)}), bf16[16,2,8064]{2,1,0:T(2,128)(2,1)}, u32[]{:S(2)}, u32[]{:S(2)}) async-start(bf16[16,2,8064]{2,1,0:T(2,128)(2,1)} %reshape.122), calls=%async_computation.1 | async-start | bytes 1032192 | tf_op jit(solution)/shard_map/all_to_all | solution.py:159
Sparse Core Ops, SparseCore 0:
  100.0 55.6 reduce-scatter.3
